TPU v7x, 32 devices: a whole 2x2x4 slice. The times are simulated.
32 devices in a mesh: groups: 2 (over x), expert: 16 (over z, y, core).
Axes of the slice: x: 2, y: 2, z: 4, core: 2. Of those that a mesh axis runs over, the one named last changes fastest.
Arguments:
- hidden_in: bfloat16 [256, 4096], P(('groups', 'expert')), parts along dimension 0, may hold values from -6 to 6
- queries: bfloat16 [256, 4096], P(('groups', 'expert')), parts along dimension 0, may hold values from -8 to 8
- decode_key_value: bfloat16 [256, 2, 256], P(('groups', 'expert')), parts along dimension 0, may hold values from -6 to 6
- local_kv: bfloat16 [1024, 2, 16, 256], P(('groups', 'expert')), parts along dimension 0, may hold values from -8 to 8
- page_table: int32 [256, 16], P(('groups', 'expert')), parts along dimension 0, may hold values from 0 to 31
- seq_blocks: int32 [256], P(('groups', 'expert')), parts along dimension 0, may hold values from 1 to 16
- prompt_kv: bfloat16 [32, 16, 2, 16, 256], P(('groups', 'expert')), parts along dimension 0, may hold values from -8 to 8
- prompt_owner: int32 [32], P('groups'), parts along dimension 0, may hold values from 0 to 15, as said below
- prompt_pages: int32 [32], P('groups'), parts along dimension 0, may hold values from 1 to 16
- norm_gain: float32 [4096], replicated, may hold values from 0.5 to 1.5
- router: bfloat16 [4096, 8], replicated, may hold values from -0.09375 to 0.09375
- w_gate: bfloat16 [16, 4096, 384], P('expert'), may hold values from -0.09375 to 0.09375
- w_up: bfloat16 [16, 4096, 384], P('expert'), may hold values from -0.09375 to 0.09375
- w_down: bfloat16 [16, 384, 4096], P('expert'), may hold values from -0.21875 to 0.21875
- route_ids: int32 [256, 8], P(('groups', 'expert')), parts along dimension 0, may hold values from 0 to 7, as said below
Outputs:
- layer_out: bfloat16 [256, 4096], P(('groups', 'expert')), parts along dimension 0
There are 2 independent parts, one for each index of `groups`. A program takes and returns all parts, laid end to end along the dimension named above; an argument that names none is the same for every part. Nothing has to cross between parts.
Inputs may be any that keep to these rules, and one draw needn't show every extreme that they name: `prompt_owner`: each device is named by at most 2 prompts, and by exactly 2 for some of the devices. `route_ids`: each row names 8 different experts; among the rows of one device no expert is named more than 8 times, a bound that some block reaches. `page_table`: indices among the pages of the sequence's own device.
All inputs are finite; a program needn't handle non-finite values.
Results may differ from a plain program's by a relative error of at most 0.0056.
Values may be sent and summed in bfloat16 or wider, within the bound.
No kernel may reach another device: no remote copies, remote signals or barrier semaphores. Data moves between devices by JAX's collectives and lax.ppermute only.
A program may use at most 128 MiB of HBM per device.

v0:
```python
import math
import jax
import jax.numpy as jnp
from jax import lax
from jax.sharding import PartitionSpec as P

D = 4096
QUERY_HEADS = 32
KEY_VALUE_HEADS = 2
HEAD_SIZE = 128
PAGE_TOKENS = 16
TOPK = 8
MAXB = 16
MAXP = 2
norm_eps = 1e-06
masked_score = -1e30


def partner(x, axis, apart):
    return lax.ppermute(x, axis, [(i, i ^ 1 << apart) for i in range(lax.axis_size(axis))])


def attend(rows_of_queries, rows_of_keys, rows_of_values, allowed, token_own_key, token_own_value):
    decode_tokens = rows_of_queries.shape[0]
    heads_of_queries = rows_of_queries.reshape(
        decode_tokens, KEY_VALUE_HEADS, QUERY_HEADS // KEY_VALUE_HEADS, HEAD_SIZE
    )
    heads_of_keys = rows_of_keys.reshape(decode_tokens, -1, KEY_VALUE_HEADS, HEAD_SIZE)
    heads_of_values = rows_of_values.reshape(decode_tokens, -1, KEY_VALUE_HEADS, HEAD_SIZE)
    scale_for_scores = 1.0 / math.sqrt(HEAD_SIZE)
    allowed_mask = allowed[:, None, None, :]
    scores = (
        jnp.einsum(
            "tkgd,tlkd->tkgl", heads_of_queries, heads_of_keys, preferred_element_type=jnp.float32
        )
        * scale_for_scores
    )
    scores = jnp.where(allowed_mask, scores, masked_score)
    token_own_score = (
        jnp.einsum(
            "xejp,xep->xej",
            heads_of_queries,
            token_own_key.reshape(decode_tokens, KEY_VALUE_HEADS, HEAD_SIZE),
            preferred_element_type=jnp.float32,
        )
        * scale_for_scores
    )
    peak = jnp.maximum(jnp.max(scores, -1), token_own_score)
    weights = jnp.where(allowed_mask, jnp.exp(scores - peak[..., None]), 0.0)
    own_weight = jnp.exp(token_own_score - peak)
    denominator = jnp.sum(weights, -1) + own_weight
    probs = (weights / denominator[..., None]).astype(jnp.bfloat16)
    token_own_probability = (own_weight / denominator).astype(jnp.bfloat16)
    blended_noise = jnp.einsum(
        "tkgl,tlkd->tkgd", probs, heads_of_values, preferred_element_type=jnp.float32
    )
    blended_noise = blended_noise + token_own_probability.astype(jnp.float32)[
        ..., None
    ] * token_own_value.reshape(decode_tokens, KEY_VALUE_HEADS, 1, HEAD_SIZE).astype(jnp.float32)
    return blended_noise.reshape(decode_tokens, QUERY_HEADS * HEAD_SIZE).astype(jnp.bfloat16)


def all_tokens(resid_wide, normed, spread, w_gate, w_up, w_down):
    devices = lax.axis_size("expert")
    seq_dev, experts = spread.shape
    expert = lax.axis_index("expert") // 2
    bits = devices.bit_length() - 1
    coarse = lax.reduce_precision(spread, 8, 7)
    fine = spread - coarse
    pad = -2 * experts % 128
    tail = jnp.pad(jnp.concatenate([coarse, fine], 1), ((0, 0), (0, pad))).astype(jnp.bfloat16)
    rows = jnp.concatenate([normed, tail], 1)
    for bit in reversed(range(bits)):
        rows = jnp.concatenate([rows, partner(rows, "expert", bit)], 0)
    gates = rows[:, D : D + 2 * experts].astype(jnp.float32).reshape(-1, 2, experts)
    own = jnp.arange(experts, dtype=jnp.int32) == expert
    gate = jnp.sum(jnp.where(own, gates, 0.0), (1, 2))
    tokens = rows[:, :D]
    gate_proj = jnp.dot(tokens, w_gate, preferred_element_type=jnp.float32)
    up_proj = jnp.dot(tokens, w_up, preferred_element_type=jnp.float32)
    activated = (jax.nn.silu(gate_proj) * up_proj).astype(jnp.bfloat16)
    mixed = jnp.dot(activated, w_down, preferred_element_type=jnp.float32) * gate[:, None]
    for bit in range(bits):
        half = mixed.shape[0] // 2
        moved = partner(mixed[half:].astype(jnp.bfloat16), "expert", bit)
        mixed = mixed[:half] + moved.astype(jnp.float32)
    return (resid_wide + mixed).astype(jnp.bfloat16)


def local(
    hidden_in,
    queries,
    decode_key_value,
    local_kv,
    page_table,
    seq_blocks,
    prompt_kv,
    prompt_owner,
    prompt_pages,
    norm_gain,
    router,
    w_gate,
    w_up,
    w_down,
    route_ids,
):
    devices = lax.axis_size("expert")
    position = lax.axis_index("expert")
    experts = devices // 2
    seq_dev = hidden_in.shape[0]
    key_value_width = KEY_VALUE_HEADS * HEAD_SIZE
    capacity = min(seq_dev, max(2, 2 * ((3 * seq_dev * TOPK + 2 * devices - 1) // (2 * devices))))
    half_cap = capacity // 2
    even_core = position % 2 == 0
    prompt_count = prompt_owner.shape[0]
    prompt_range = jnp.arange(prompt_count, dtype=jnp.int32)
    same_owner = prompt_owner[:, None] == prompt_owner[None, :]
    earlier = prompt_range[None, :] < prompt_range[:, None]
    arrival = jnp.sum((same_owner & earlier).astype(jnp.int32), 1)
    matching = (
        prompt_owner[None, None, :] == jnp.arange(devices, dtype=jnp.int32)[:, None, None]
    ) & (arrival[None, None, :] == jnp.arange(MAXP, dtype=jnp.int32)[None, :, None])
    chosen_prompt = jnp.sum(jnp.where(matching, prompt_range[None, None, :], 0), -1)
    occupied = jnp.any(matching, -1)
    own_picks = lax.dynamic_index_in_dim(chosen_prompt, position, 0, keepdims=False)
    own_occupied = lax.dynamic_index_in_dim(occupied, position, 0, keepdims=False)
    page_rows = prompt_kv[0]
    outgoing = jnp.take(page_rows, chosen_prompt.T.reshape(-1), axis=0).reshape(
        MAXP, devices, 2, PAGE_TOKENS, key_value_width
    )
    outgoing = jnp.where(occupied.T[:, :, None, None, None], outgoing, 0)
    arrived = lax.all_to_all(outgoing, "expert", split_axis=1, concat_axis=1, tiled=True)
    lengths = jnp.take(prompt_pages, own_picks)
    new_keys = arrived[:, :, 0].reshape(MAXP, devices * PAGE_TOKENS, key_value_width)
    new_values = arrived[:, :, 1].reshape(MAXP, devices * PAGE_TOKENS, key_value_width)
    new_allowed = (jnp.arange(devices * PAGE_TOKENS, dtype=jnp.int32) // PAGE_TOKENS)[
        None, :
    ] < lengths[:, None]
    fresh_rows = attend(
        queries[:MAXP],
        new_keys,
        new_values,
        new_allowed,
        decode_key_value[:MAXP, 0],
        decode_key_value[:MAXP, 1],
    )
    fetched = local_kv[page_table]
    old_keys = fetched[:, :, 0].reshape(seq_dev, MAXB * PAGE_TOKENS, key_value_width)
    old_values = fetched[:, :, 1].reshape(seq_dev, MAXB * PAGE_TOKENS, key_value_width)
    old_allowed = (jnp.arange(MAXB * PAGE_TOKENS, dtype=jnp.int32) // PAGE_TOKENS)[
        None, :
    ] < seq_blocks[:, None]
    old_out = attend(
        queries, old_keys, old_values, old_allowed, decode_key_value[:, 0], decode_key_value[:, 1]
    )
    new_count = jnp.sum(own_occupied.astype(jnp.int32))
    is_new = jnp.arange(MAXP, dtype=jnp.int32) < new_count
    attention = jnp.concatenate(
        [jnp.where(is_new[:, None], fresh_rows, old_out[:MAXP]), old_out[MAXP:]], 0
    )
    residual = (hidden_in.astype(jnp.float32) + attention.astype(jnp.float32)).astype(jnp.bfloat16)
    resid_wide = residual.astype(jnp.float32)
    normed = (
        resid_wide
        * lax.rsqrt(jnp.mean(resid_wide * resid_wide, -1, keepdims=True) + norm_eps)
        * norm_gain
    ).astype(jnp.bfloat16)
    logits = jnp.dot(normed, router, preferred_element_type=jnp.float32)
    expert_onehot = route_ids[:, :, None] == jnp.arange(experts, dtype=jnp.int32)[None, None, :]
    selected = jnp.sum(jnp.where(expert_onehot, logits[:, None, :], 0.0), -1)
    gate_weights = jax.nn.softmax(selected, -1)
    if capacity >= seq_dev and devices & devices - 1 == 0:
        spread = jnp.sum(jnp.where(expert_onehot, gate_weights[:, :, None], 0.0), 1)
        return all_tokens(resid_wide, normed, spread, w_gate[0], w_up[0], w_down[0])
    assigned = seq_dev * TOPK
    expert_ids = route_ids.reshape(assigned)
    chosen = (expert_ids[:, None] == jnp.arange(experts, dtype=jnp.int32)[None, :]).astype(
        jnp.int32
    )
    before = jnp.cumsum(chosen, 0) - chosen
    slot_rank = jnp.sum(before * chosen, 1)
    slot_index = expert_ids * capacity + slot_rank
    placing = slot_index[None, :] == jnp.arange(experts * capacity, dtype=jnp.int32)[:, None]
    selector = jnp.any(placing.reshape(experts * capacity, seq_dev, TOPK), -1).astype(jnp.bfloat16)
    gathered_rows = jnp.dot(selector, normed, preferred_element_type=jnp.float32).astype(
        jnp.bfloat16
    )
    outgoing_half = gathered_rows.reshape(devices, half_cap, D)
    own_half = lax.all_to_all(outgoing_half, "expert", split_axis=0, concat_axis=0, tiled=True)
    partner_half = partner(own_half, "expert", 0)
    received = jnp.where(
        even_core,
        jnp.concatenate([own_half, partner_half], 1),
        jnp.concatenate([partner_half, own_half], 1),
    )
    flattened = received.reshape(devices * capacity, D)
    gate_proj = jnp.dot(flattened, w_gate[0], preferred_element_type=jnp.float32)
    up_proj = jnp.dot(flattened, w_up[0], preferred_element_type=jnp.float32)
    activated = (jax.nn.silu(gate_proj) * up_proj).astype(jnp.bfloat16)
    partial_value = jnp.dot(activated, w_down[0], preferred_element_type=jnp.float32).reshape(
        devices, capacity, D
    )
    kept = jnp.where(even_core, partial_value[:, :half_cap], partial_value[:, half_cap:])
    handed = jnp.where(even_core, partial_value[:, half_cap:], partial_value[:, :half_cap])
    partner_part = partner(handed, "expert", 0)
    finished = (kept + partner_part).astype(jnp.bfloat16)
    returned = lax.all_to_all(finished, "expert", split_axis=0, concat_axis=0, tiled=True)
    expert_sum = returned.reshape(experts * capacity, D)
    picked = jnp.take(expert_sum, slot_index, axis=0).astype(jnp.float32).reshape(seq_dev, TOPK, D)
    expert_mix = jnp.sum(picked * gate_weights[:, :, None], 1)
    return (resid_wide + expert_mix).astype(jnp.bfloat16)


def solution(mesh):
    return jax.shard_map(
        local,
        mesh=mesh,
        in_specs=(
            P(("groups", "expert"), None),
            P(("groups", "expert"), None),
            P(("groups", "expert"), None, None),
            P(("groups", "expert"), None, None, None),
            P(("groups", "expert"), None),
            P(("groups", "expert")),
            P(("groups", "expert"), None, None, None, None),
            P("groups"),
            P("groups"),
            P(),
            P(),
            P("expert", None, None),
            P("expert", None, None),
            P("expert", None, None),
            P(("groups", "expert"), None),
        ),
        out_specs=P(("groups", "expert"), None),
        check_vma=False,
    )
```

profile of v0, /device:TPU:0, one launch (start us, length us, event | category | flops | bytes accessed | tf_op | source)
XLA Modules:
  0.0 98.2 jit_solution(18162269884148207099)
XLA Ops:
  0.0 1.0 %convert_reduce_fusion = s32[16]{0:T(128)S(1)} fusion(s32[16]{0:T(128)} %param.22), kind=kLoop, calls=%fused_computation.86 | loop fusion | flops 1264 | bytes 128 | tf_op jit(solution)/shard_map/reduce_sum | solution.py:119
  2.8 2.3 %gather_fusion.1 = bf16[32,2,16,256]{3,2,1,0:T(8,128)(2,1)} fusion(bf16[16,2,16,256]{3,2,1,0:T(8,128)(2,1)} %bitcast.87, s32[1024]{0:T(1024)S(1)} %get-tuple-element.26), kind=kCustom, calls=%fused_computation.1 | custom fusion | bytes 1048704 | tf_op jit(solution)/shard_map/jit(_take)/gather | solution.py:128
  5.1 1.2 %select_select_fusion = bf16[2,16,2,16,256]{4,3,2,1,0:T(8,128)(2,1)S(1)} fusion(bf16[2,16,2,16,256]{4,3,2,1,0:T(8,128)(2,1)} %bitcast.86, pred[2,16]{1,0:T(4,128)(4,1)S(1)} %compare_and_fusion, pred[2,16]{1,0:T(4,128)(4,1)S(1)} %bitcast.99), kind=kLoop, calls=%fused_computation.30 | loop fusion | flops 524288 | bytes 1048640 | tf_op jit(solution)/shard_map/jit(_where)/select_n | solution.py:131
  6.3 0.9 copy.48
  7.2 7.5 %all-to-all-start = ((bf16[2,16,2,16,256]{4,3,0,2,1:T(8,128)(2,1)}), bf16[2,16,2,16,256]{4,3,0,2,1:T(8,128)(2,1)}, u32[]{:S(2)}, u32[]{:S(2)}) async-start(bf16[2,16,2,16,256]{4,3,0,2,1:T(8,128)(2,1)} %copy.48), calls=%async_computation | async-start | bytes 1048576 | tf_op jit(solution)/shard_map/all_to_all | solution.py:132
  14.7 3.1 %gather_fusion.2 = bf16[128,2,16,256]{3,2,1,0:T(8,128)(2,1)} fusion(bf16[32,2,16,256]{3,2,1,0:T(8,128)(2,1)} %param.18, s32[1024]{0:T(1024)S(1)} %get-tuple-element.25), kind=kCustom, calls=%fused_computation.2 | custom fusion | bytes 4194816 | tf_op jit(solution)/shard_map/gather | solution.py:147
  17.8 3.0 %slice_bitcast_fusion.1 = (bf16[8,16,1,16,256]{4,3,1,0,2:T(8,128)(2,1)}, bf16[8,16,1,16,256]{4,3,1,0,2:T(8,128)(2,1)}) fusion(bf16[8,16,2,16,256]{4,3,2,1,0:T(8,128)(2,1)} %bitcast.85), kind=kLoop, calls=%fused_computation.22 | loop fusion | bytes 4194304
  20.8 2.2 %reshape_reshape_squeeze.15 = bf16[8,256,2,128]{3,2,1,0:T(2,128)(2,1)} reshape(bf16[8,16,1,16,256]{4,3,1,0,2:T(8,128)(2,1)} %get-tuple-element.8) | data formatting | bytes 2097152 | tf_op jit(solution)/shard_map/reshape;reshape;squeeze | solution.py:29
  23.0 2.2 %reshape_reshape_squeeze.14 = bf16[8,256,2,128]{3,2,1,0:T(2,128)(2,1)} reshape(bf16[8,16,1,16,256]{4,3,1,0,2:T(8,128)(2,1)} %get-tuple-element.7) | data formatting | bytes 2097152 | tf_op jit(solution)/shard_map/reshape;reshape;squeeze | solution.py:28
  25.5 1.8 %fusion.66 = (f32[8,2,16]{2,1,0:T(2,128)S(1)}, f32[8,2,16,256]{3,2,1,0:T(8,128)S(1)}) fusion(bf16[8,2,16,128]{3,0,2,1:T(8,128)(2,1)S(1)} %bitcast.103, bf16[8,256,2,128]{3,2,1,0:T(2,128)(2,1)} %reshape_reshape_squeeze.14, pred[8,256]{1,0:T(8,128)(4,1)S(1)} %broadcast_compare_fusion), kind=kOutput, calls=%fused_computation.142 | convolution fusion | flops 16973568 | bytes 1379328 | tf_op jit(solution)/shard_map/tkgd,tlkd->tkgl/dot_general | solution.py:33
  29.4 1.1 %iota_compare_fusion.6 = pred[2]{0:T(512)(128)(4,1)} fusion(s32[]{:T(128)} %get-tuple-element.27), kind=kLoop, calls=%fused_computation.135 | loop fusion | flops 2 | bytes 6 | tf_op jit(solution)/shard_map/lt | solution.py:157
  32.4 1.8 %fusion.65 = (bf16[2,16,1,16,256]{4,3,0,2,1:T(8,128)(2,1)}, bf16[2,16,1,16,256]{4,3,0,2,1:T(8,128)(2,1)S(1)}) fusion(bf16[2,16,2,16,256]{4,3,0,2,1:T(8,128)(2,1)} %all-to-all-done), kind=kLoop, calls=%fused_computation.141 | loop fusion | bytes 1048576 | tf_op jit(solution)/shard_map/slice | solution.py:134
  34.9 1.0 %copy.49 = bf16[2,16,1,16,256]{4,3,1,0,2:T(8,128)(2,1)S(1)} copy(bf16[2,16,1,16,256]{4,3,0,2,1:T(8,128)(2,1)} %get-tuple-element.9) | data formatting | bytes 524288 | tf_op jit(solution)/shard_map/slice | solution.py:134
  36.7 1.3 %fusion.67 = (f32[2,2,16]{2,1,0:T(2,128)S(1)}, f32[2,2,16,256]{3,2,1,0:T(8,128)S(1)}) fusion(bf16[2,2,16,128]{3,2,1,0:T(8,128)(2,1)} %bitcast.95, bf16[2,256,2,128]{3,2,1,0:T(2,128)(2,1)} %reshape_reshape_squeeze.12, pred[2,256]{1,0:T(4,128)(4,1)} %broadcast_compare_fusion.1), kind=kOutput, calls=%fused_computation.143 | convolution fusion | flops 4243392 | bytes 344832 | tf_op jit(solution)/shard_map/tkgd,tlkd->tkgl/dot_general | solution.py:33
  40.1 1.2 %fusion.10 = bf16[2,2,16,128]{3,2,1,0:T(8,128)(2,1)S(1)} fusion(bf16[2,256,2,128]{3,2,1,0:T(2,128)(2,1)} %reshape_reshape_squeeze.13, f32[2,2,16,256]{3,2,1,0:T(8,128)S(1)} %get-tuple-element.24, f32[2,2,16]{2,1,0:T(2,128)S(1)} %get-tuple-element.18, f32[2,2,16]{2,1,0:T(2,128)S(1)} %multiply_maximum_fusion.1, pred[2,256]{1,0:T(4,128)(4,1)} %broadcast_compare_fusion.1, ...), kind=kOutput, calls=%fused_computation.18 | convolution fusion | flops 4284416 | bytes 347392 | tf_op jit(solution)/shard_map/tkgl,tlkd->tkgd/dot_general | solution.py:54
  43.9 2.8 %collective-permute-start = (bf16[8,4224]{1,0:T(8,128)(2,1)S(1)}, bf16[8,4224]{1,0:T(8,128)(2,1)S(1)}, u32[]{:S(2)}, u32[]{:S(2)}) collective-permute-start(bf16[8,4224]{1,0:T(8,128)(2,1)S(1)} %get-tuple-element.11), channel_id=1, source_target_pairs={{0,8},{1,9},{2,10},{3,11},{4,12},{5,13},{6,14},{7,15},{8,0},{9,1},... | collective-permute-start | bytes 202760 | tf_op jit(solution)/shard_map/ppermute | solution.py:20
  46.8 3.9 %collective-permute-done = bf16[8,4224]{1,0:T(8,128)(2,1)S(1)} collective-permute-done((bf16[8,4224]{1,0:T(8,128)(2,1)S(1)}, bf16[8,4224]{1,0:T(8,128)(2,1)S(1)}, u32[]{:S(2)}, u32[]{:S(2)}) %collective-permute-start) | collective-permute-done | bytes 67616 | tf_op jit(solution)/shard_map/ppermute | solution.py:20
  52.0 3.8 %collective-permute-done.1 = bf16[16,4224]{1,0:T(8,128)(2,1)S(1)} collective-permute-done((bf16[16,4224]{1,0:T(8,128)(2,1)S(1)}, bf16[16,4224]{1,0:T(8,128)(2,1)S(1)}, u32[]{:S(2)}, u32[]{:S(2)}) %collective-permute-start.1) | collective-permute-done | bytes 135200 | tf_op jit(solution)/shard_map/ppermute | solution.py:20
  55.8 1.8 %collective-permute-start.2 = (bf16[32,4224]{1,0:T(8,128)(2,1)S(1)}, bf16[32,4224]{1,0:T(8,128)(2,1)S(1)}, u32[]{:S(2)}, u32[]{:S(2)}) collective-permute-start(bf16[32,4224]{1,0:T(8,128)(2,1)S(1)} %pad_maximum_fusion.1), channel_id=1, source_target_pairs={{0,2},{1,3},{2,0},{3,1},{4,6},{5,7},{6,4},{7,5},{8,10},{9,11},{10,... | collective-permute-start | bytes 811016 | tf_op jit(solution)/shard_map/ppermute | solution.py:20
  58.3 4.0 %collective-permute-done.2 = bf16[32,4224]{1,0:T(8,128)(2,1)S(1)} collective-permute-done((bf16[32,4224]{1,0:T(8,128)(2,1)S(1)}, bf16[32,4224]{1,0:T(8,128)(2,1)S(1)}, u32[]{:S(2)}, u32[]{:S(2)}) %collective-permute-start.2) | collective-permute-done | bytes 270368 | tf_op jit(solution)/shard_map/ppermute | solution.py:20
  63.2 1.2 %collective-permute-done.3 = bf16[64,4224]{1,0:T(8,128)(2,1)S(1)} collective-permute-done((bf16[64,4224]{1,0:T(8,128)(2,1)S(1)}, bf16[64,4224]{1,0:T(8,128)(2,1)S(1)}, u32[]{:S(2)}, u32[]{:S(2)}) %collective-permute-start.3) | collective-permute-done | bytes 540704 | tf_op jit(solution)/shard_map/ppermute | solution.py:20
  66.1 1.9 %fusion.1 = f32[128,384]{1,0:T(8,128)S(1)} fusion(bf16[1,4096,384]{2,1,0:T(8,128)(2,1)S(1)} %copy-done.2, bf16[128,4224]{1,0:T(8,128)(2,1)} %constant_dynamic-update-slice_fusion), kind=kOutput, calls=%fused_computation.5 | convolution fusion | flops 402653184 | bytes 4390912 | tf_op jit(solution)/shard_map/dot_general | solution.py:80
  68.0 5.0 %convolution_multiply_fusion = f32[128,4096]{1,0:T(8,128)} fusion(bf16[1,384,4096]{2,1,0:T(8,128)(2,1)S(1)} %copy-done, f32[128]{0:T(128)S(1)} %select_reduce_fusion, f32[128,384]{1,0:T(8,128)S(1)} %fusion.1, bf16[1,4096,384]{2,1,0:T(8,128)(2,1)} %param.26, bf16[128,4224]{1,0:T(8,128)(2,1)} %constant_dynamic-update-slice_fusion), kind=kOutput, calls=%fused_computation.3 | convolution fusion | flops 806125568 | bytes 9634304 | tf_op jit(solution)/shard_map/dot_general | solution.py:82
  73.0 1.3 %slice.146 = bf16[64,4096]{1,0:T(8,128)(2,1)S(1)} slice(f32[128,4096]{1,0:T(8,128)} %convolution_multiply_fusion), slice={[64:128], [0:4096]} | slice | bytes 1048576 | tf_op jit(solution)/shard_map/slice | solution.py:85
  74.5 1.8 %collective-permute-done.4 = bf16[64,4096]{1,0:T(8,128)(2,1)S(1)} collective-permute-done((bf16[64,4096]{1,0:T(8,128)(2,1)S(1)}, bf16[64,4096]{1,0:T(8,128)(2,1)S(1)}, u32[]{:S(2)}, u32[]{:S(2)}) %collective-permute-start.4) | collective-permute-done | bytes 524320 | tf_op jit(solution)/shard_map/ppermute | solution.py:20
  76.3 1.3 %slice_add_fusion = f32[64,4096]{1,0:T(8,128)S(1)} fusion(f32[128,4096]{1,0:T(8,128)} %convolution_multiply_fusion, bf16[64,4096]{1,0:T(8,128)(2,1)S(1)} %collective-permute-done.4), kind=kLoop, calls=%fused_computation.20 | loop fusion | flops 524288 | bytes 2621440 | tf_op jit(solution)/shard_map/add | solution.py:86
  77.6 1.8 %collective-permute-start.5 = (bf16[32,4096]{1,0:T(8,128)(2,1)S(1)}, bf16[32,4096]{1,0:T(8,128)(2,1)S(1)}, u32[]{:S(2)}, u32[]{:S(2)}) collective-permute-start(bf16[32,4096]{1,0:T(8,128)(2,1)S(1)} %slice.147), channel_id=1, source_target_pairs={{0,2},{1,3},{2,0},{3,1},{4,6},{5,7},{6,4},{7,5},{8,10},{9,11},{10,... | collective-permute-start | bytes 786440 | tf_op jit(solution)/shard_map/ppermute | solution.py:20
  79.4 6.6 %collective-permute-done.5 = bf16[32,4096]{1,0:T(8,128)(2,1)S(1)} collective-permute-done((bf16[32,4096]{1,0:T(8,128)(2,1)S(1)}, bf16[32,4096]{1,0:T(8,128)(2,1)S(1)}, u32[]{:S(2)}, u32[]{:S(2)}) %collective-permute-start.5) | collective-permute-done | bytes 262176 | tf_op jit(solution)/shard_map/ppermute | solution.py:20
  86.1 2.2 %collective-permute-start.6 = (bf16[16,4096]{1,0:T(8,128)(2,1)S(1)}, bf16[16,4096]{1,0:T(8,128)(2,1)S(1)}, u32[]{:S(2)}, u32[]{:S(2)}) collective-permute-start(bf16[16,4096]{1,0:T(8,128)(2,1)S(1)} %slice.148), channel_id=1, source_target_pairs={{0,4},{1,5},{2,6},{3,7},{4,0},{5,1},{6,2},{7,3},{8,12},{9,13},{10,... | collective-permute-start | bytes 393224 | tf_op jit(solution)/shard_map/ppermute | solution.py:20
  88.3 2.9 %collective-permute-done.6 = bf16[16,4096]{1,0:T(8,128)(2,1)S(1)} collective-permute-done((bf16[16,4096]{1,0:T(8,128)(2,1)S(1)}, bf16[16,4096]{1,0:T(8,128)(2,1)S(1)}, u32[]{:S(2)}, u32[]{:S(2)}) %collective-permute-start.6) | collective-permute-done | bytes 131104 | tf_op jit(solution)/shard_map/ppermute | solution.py:20
  91.3 4.0 %collective-permute-start.7 = (bf16[8,4096]{1,0:T(8,128)(2,1)S(1)}, bf16[8,4096]{1,0:T(8,128)(2,1)S(1)}, u32[]{:S(2)}, u32[]{:S(2)}) collective-permute-start(bf16[8,4096]{1,0:T(8,128)(2,1)S(1)} %slice.149), channel_id=1, source_target_pairs={{0,8},{1,9},{2,10},{3,11},{4,12},{5,13},{6,14},{7,15},{8,0},{9,1},... | collective-permute-start | bytes 196616 | tf_op jit(solution)/shard_map/ppermute | solution.py:20
  95.3 2.2 %collective-permute-done.7 = bf16[8,4096]{1,0:T(8,128)(2,1)S(1)} collective-permute-done((bf16[8,4096]{1,0:T(8,128)(2,1)S(1)}, bf16[8,4096]{1,0:T(8,128)(2,1)S(1)}, u32[]{:S(2)}, u32[]{:S(2)}) %collective-permute-start.7) | collective-permute-done | bytes 65568 | tf_op jit(solution)/shard_map/ppermute | solution.py:20
  (101 shorter events, 17.9 us)
Async XLA Ops:
  0.0 68.0 %copy-start = (bf16[1,384,4096]{2,1,0:T(8,128)(2,1)S(1)}, bf16[1,384,4096]{2,1,0:T(8,128)(2,1)}, u32[]{:S(2)}) copy-start(bf16[1,384,4096]{2,1,0:T(8,128)(2,1)} %param.28) | copy-start | bytes 9437188
  7.2 25.2 %all-to-all-start = ((bf16[2,16,2,16,256]{4,3,0,2,1:T(8,128)(2,1)}), bf16[2,16,2,16,256]{4,3,0,2,1:T(8,128)(2,1)}, u32[]{:S(2)}, u32[]{:S(2)}) async-start(bf16[2,16,2,16,256]{4,3,0,2,1:T(8,128)(2,1)} %copy.48), calls=%async_computation | async-start | bytes 1048576 | tf_op jit(solution)/shard_map/all_to_all | solution.py:132
  23.0 2.2 %copy-start.7 = (bf16[8,2,256]{2,1,0:T(2,128)(2,1)S(1)}, bf16[8,2,256]{2,1,0:T(2,128)(2,1)}, u32[]{:S(2)}) copy-start(bf16[8,2,256]{2,1,0:T(2,128)(2,1)} %param.17) | copy-start | bytes 24580
  23.0 2.3 %copy-start.13 = (s32[8]{0:T(128)S(1)}, s32[8]{0:T(128)}, u32[]{:S(2)}) copy-start(s32[8]{0:T(128)} %param.20) | copy-start | bytes 100
  23.0 2.4 %copy-start.11 = (bf16[8,4096]{1,0:T(8,128)(2,1)S(1)}, bf16[8,4096]{1,0:T(8,128)(2,1)}, u32[]{:S(2)}) copy-start(bf16[8,4096]{1,0:T(8,128)(2,1)} %param.16) | copy-start | bytes 196612
  25.5 2.1 %copy-start.3 = (bf16[8,256,2,128]{3,2,1,0:T(2,128)(2,1)S(1)}, bf16[8,256,2,128]{3,2,1,0:T(2,128)(2,1)}, u32[]{:S(2)}) copy-start(bf16[8,256,2,128]{3,2,1,0:T(2,128)(2,1)} %reshape_reshape_squeeze.15) | copy-start | bytes 3145732
  27.5 1.2 %copy-start.1 = (s32[16]{0:T(128)S(1)}, s32[16]{0:T(128)}, u32[]{:S(2)}) copy-start(s32[16]{0:T(128)} %param.23) | copy-start | bytes 196
  27.9 6.3 %copy-start.4 = (bf16[8,2,16,128]{3,2,1,0:T(8,128)(2,1)}, bf16[8,2,16,128]{3,2,1,0:T(8,128)(2,1)S(1)}, u32[]{:S(2)}) copy-start(bf16[8,2,16,128]{3,2,1,0:T(8,128)(2,1)S(1)} %fusion.7) | copy-start | bytes 196612
  28.7 5.4 %copy-start.10 = (bf16[1,2,32,128]{3,2,1,0:T(8,128)(2,1)}, bf16[1,2,32,128]{3,2,1,0:T(8,128)(2,1)S(1)}, u32[]{:S(2)}) copy-start(bf16[1,2,32,128]{3,2,1,0:T(8,128)(2,1)S(1)} %copy.66) | copy-start | bytes 49156
  34.9 6.4 %slice-start = ((bf16[8,2,16,128]{3,2,1,0:T(8,128)(2,1)}), bf16[2,2,16,128]{3,2,1,0:T(8,128)(2,1)S(1)}, s32[]{:S(2)}) async-start(bf16[8,2,16,128]{3,2,1,0:T(8,128)(2,1)} %copy-done.4), calls=%async_computation.1 | async-start | bytes 32768 | tf_op jit(solution)/shard_map/slice | solution.py:159
  34.9 6.5 %copy-start.5 = (bf16[8,4096]{1,0:T(8,128)(2,1)S(1)}, bf16[8,4096]{1,0:T(8,128)(2,1)}, u32[]{:S(2)}) copy-start(bf16[8,4096]{1,0:T(8,128)(2,1)} %param.15) | copy-start | bytes 196612
  36.7 4.6 %copy-start.12 = (pred[2]{0:T(512)(128)(4,1)S(1)}, pred[2]{0:T(512)(128)(4,1)}, u32[]{:S(2)}) copy-start(pred[2]{0:T(512)(128)(4,1)} %iota_compare_fusion.6) | copy-start | bytes 10
  36.7 4.9 %copy-start.8 = (f32[4096]{0:T(1024)S(1)}, f32[4096]{0:T(1024)}, u32[]{:S(2)}) copy-start(f32[4096]{0:T(1024)} %param.24) | copy-start | bytes 49156
  36.7 5.0 %copy-start.6 = (bf16[4096,8]{0,1:T(8,128)(2,1)S(1)}, bf16[4096,8]{0,1:T(8,128)(2,1)}, u32[]{:S(2)}) copy-start(bf16[4096,8]{0,1:T(8,128)(2,1)} %param.25) | copy-start | bytes 196612
  36.7 5.2 %copy-start.9 = (s32[8,8]{1,0:T(8,128)S(1)}, s32[8,8]{1,0:T(8,128)}, u32[]{:S(2)}) copy-start(s32[8,8]{1,0:T(8,128)} %param.29) | copy-start | bytes 772
  43.9 6.7 %collective-permute-start = (bf16[8,4224]{1,0:T(8,128)(2,1)S(1)}, bf16[8,4224]{1,0:T(8,128)(2,1)S(1)}, u32[]{:S(2)}, u32[]{:S(2)}) collective-permute-start(bf16[8,4224]{1,0:T(8,128)(2,1)S(1)} %get-tuple-element.11), channel_id=1, source_target_pairs={{0,8},{1,9},{2,10},{3,11},{4,12},{5,13},{6,14},{7,15},{8,0},{9,1},... | collective-permute-start | bytes 202760 | tf_op jit(solution)/shard_map/ppermute | solution.py:20
  50.7 5.1 %collective-permute-start.1 = (bf16[16,4224]{1,0:T(8,128)(2,1)S(1)}, bf16[16,4224]{1,0:T(8,128)(2,1)S(1)}, u32[]{:S(2)}, u32[]{:S(2)}) collective-permute-start(bf16[16,4224]{1,0:T(8,128)(2,1)S(1)} %pad_maximum_fusion.2), channel_id=1, source_target_pairs={{0,4},{1,5},{2,6},{3,7},{4,0},{5,1},{6,2},{7,3},{8,12},{9,13},{10,... | collective-permute-start | bytes 405512 | tf_op jit(solution)/shard_map/ppermute | solution.py:20
  55.8 10.3 %copy-start.2 = (bf16[1,4096,384]{2,1,0:T(8,128)(2,1)S(1)}, bf16[1,4096,384]{2,1,0:T(8,128)(2,1)}, u32[]{:S(2)}) copy-start(bf16[1,4096,384]{2,1,0:T(8,128)(2,1)} %param.27) | copy-start | bytes 9437188
  55.8 6.5 %collective-permute-start.2 = (bf16[32,4224]{1,0:T(8,128)(2,1)S(1)}, bf16[32,4224]{1,0:T(8,128)(2,1)S(1)}, u32[]{:S(2)}, u32[]{:S(2)}) collective-permute-start(bf16[32,4224]{1,0:T(8,128)(2,1)S(1)} %pad_maximum_fusion.1), channel_id=1, source_target_pairs={{0,2},{1,3},{2,0},{3,1},{4,6},{5,7},{6,4},{7,5},{8,10},{9,11},{10,... | collective-permute-start | bytes 811016 | tf_op jit(solution)/shard_map/ppermute | solution.py:20
  62.4 2.0 %collective-permute-start.3 = (bf16[64,4224]{1,0:T(8,128)(2,1)S(1)}, bf16[64,4224]{1,0:T(8,128)(2,1)S(1)}, u32[]{:S(2)}, u32[]{:S(2)}) collective-permute-start(bf16[64,4224]{1,0:T(8,128)(2,1)S(1)} %pad_maximum_fusion), channel_id=1, source_target_pairs={{0,1},{1,0},{2,3},{3,2},{4,5},{5,4},{6,7},{7,6},{8,9},{9,8},{10,11... | collective-permute-start | bytes 1622024 | tf_op jit(solution)/shard_map/ppermute | solution.py:20
  74.3 2.0 %collective-permute-start.4 = (bf16[64,4096]{1,0:T(8,128)(2,1)S(1)}, bf16[64,4096]{1,0:T(8,128)(2,1)S(1)}, u32[]{:S(2)}, u32[]{:S(2)}) collective-permute-start(bf16[64,4096]{1,0:T(8,128)(2,1)S(1)} %slice.146), channel_id=1, source_target_pairs={{0,1},{1,0},{2,3},{3,2},{4,5},{5,4},{6,7},{7,6},{8,9},{9,8},{10,11... | collective-permute-start | bytes 1572872 | tf_op jit(solution)/shard_map/ppermute | solution.py:20
  77.6 8.4 %collective-permute-start.5 = (bf16[32,4096]{1,0:T(8,128)(2,1)S(1)}, bf16[32,4096]{1,0:T(8,128)(2,1)S(1)}, u32[]{:S(2)}, u32[]{:S(2)}) collective-permute-start(bf16[32,4096]{1,0:T(8,128)(2,1)S(1)} %slice.147), channel_id=1, source_target_pairs={{0,2},{1,3},{2,0},{3,1},{4,6},{5,7},{6,4},{7,5},{8,10},{9,11},{10,... | collective-permute-start | bytes 786440 | tf_op jit(solution)/shard_map/ppermute | solution.py:20
  86.1 5.1 %collective-permute-start.6 = (bf16[16,4096]{1,0:T(8,128)(2,1)S(1)}, bf16[16,4096]{1,0:T(8,128)(2,1)S(1)}, u32[]{:S(2)}, u32[]{:S(2)}) collective-permute-start(bf16[16,4096]{1,0:T(8,128)(2,1)S(1)} %slice.148), channel_id=1, source_target_pairs={{0,4},{1,5},{2,6},{3,7},{4,0},{5,1},{6,2},{7,3},{8,12},{9,13},{10,... | collective-permute-start | bytes 393224 | tf_op jit(solution)/shard_map/ppermute | solution.py:20
  91.3 6.2 %collective-permute-start.7 = (bf16[8,4096]{1,0:T(8,128)(2,1)S(1)}, bf16[8,4096]{1,0:T(8,128)(2,1)S(1)}, u32[]{:S(2)}, u32[]{:S(2)}) collective-permute-start(bf16[8,4096]{1,0:T(8,128)(2,1)S(1)} %slice.149), channel_id=1, source_target_pairs={{0,8},{1,9},{2,10},{3,11},{4,12},{5,13},{6,14},{7,15},{8,0},{9,1},... | collective-permute-start | bytes 196616 | tf_op jit(solution)/shard_map/ppermute | solution.py:20
where the time goes:
time: 99.1 us; the launch traced here: 98.2 us
  waiting for transfers between devices  26.4 us (27%)
  local copies, waits for them, and re-layouts  23.2 us (23%)
  starting transfers between devices  21 us (21%)
  other arithmetic  14.7 us (15%)
  matrix products  12.4 us (13%)
    ppermute x8, waiting for transfers between devices, partner(): lax.ppermute(x, axis, [(i, i ^ 1 << apart) for i in range(lax.axis_size(a...  26.4 us
    ppermute x8, starting transfers between devices, partner(): lax.ppermute(x, axis, [(i, i ^ 1 << apart) for i in range(lax.axis_size(a...  13.6 us
    all_to_all x1, starting transfers between devices, local(): lax.all_to_all(outgoing, 'expert', split_axis=1, concat_axis=1, tiled=True)  7.46 us
    unnamed x36, local copies, waits for them, and re-layouts  5.18 us
    dot_general x1, matrix products, all_tokens(): jnp.dot(activated, w_down, preferred_element_type=jnp.float32)  4.98 us
    gather x1, local copies, waits for them, and re-layouts, local(): fetched = local_kv[page_table]  3.07 us
    dot_general x2, matrix products, attend(): jnp.einsum('tkgd,tlkd->tkgl', heads_of_queries, heads_of_keys, preferred_...  3.04 us
    another operation x2, local copies, waits for them, and re-layouts, attend(): rows_of_keys.reshape(decode_tokens, -1, KEY_VALUE_HEADS, HEAD_SIZE)  3 us
  transfers between devices with their start and end apart: 9, of which 8 were waited for; matrix products, arithmetic and copies ran while one was open for 20% of the time, Pallas kernels for 0%

commit v1 on v0

--- a/solution.py
+++ b/solution.py
@@ -14,6 +14,16 @@
 MAXP = 2
 norm_eps = 1e-06
 masked_score = -1e30
+
+
+def clear_quarters(xs, out_dim, row_dim):
+    upper = jnp.concatenate(
+        lax.all_to_all(
+            jnp.stack(jnp.split(xs, lax.psum(1, "expert"), axis=out_dim)), "expert", 0, 0
+        ),
+        axis=row_dim,
+    )
+    return upper
 
 
 def partner(x, axis, apart):
@@ -129,7 +139,7 @@
         MAXP, devices, 2, PAGE_TOKENS, key_value_width
     )
     outgoing = jnp.where(occupied.T[:, :, None, None, None], outgoing, 0)
-    arrived = lax.all_to_all(outgoing, "expert", split_axis=1, concat_axis=1, tiled=True)
+    arrived = clear_quarters(outgoing, out_dim=1, row_dim=1)
     lengths = jnp.take(prompt_pages, own_picks)
     new_keys = arrived[:, :, 0].reshape(MAXP, devices * PAGE_TOKENS, key_value_width)
     new_values = arrived[:, :, 1].reshape(MAXP, devices * PAGE_TOKENS, key_value_width)

time: 99.1 us -> 99.3 us (level)
    unnamed x36 -> x51, local copies, waits for them, and re-layouts: 5.18 us -> 5.25 us
where the time goes in v1:
time: 99.3 us; the launch traced here: 98.4 us
  waiting for transfers between devices  26.4 us (27%)
  local copies, waits for them, and re-layouts  23.3 us (23%)
  starting transfers between devices  21 us (21%)
  other arithmetic  14.7 us (15%)
  matrix products  12.4 us (12%)
    ppermute x8, waiting for transfers between devices, partner(): lax.ppermute(x, axis, [(i, i ^ 1 << apart) for i in range(lax.axis_size(a...  26.4 us
    ppermute x8, starting transfers between devices, partner(): lax.ppermute(x, axis, [(i, i ^ 1 << apart) for i in range(lax.axis_size(a...  13.6 us
    all_to_all x1, starting transfers between devices, clear_quarters(): lax.all_to_all(jnp.stack(jnp.split(xs, lax.psum(1, 'expert'), axis=out_di...  7.46 us
    unnamed x51, local copies, waits for them, and re-layouts  5.25 us
    dot_general x1, matrix products, all_tokens(): jnp.dot(activated, w_down, preferred_element_type=jnp.float32)  4.98 us
    gather x1, local copies, waits for them, and re-layouts, local(): fetched = local_kv[page_table]  3.07 us
    dot_general x2, matrix products, attend(): jnp.einsum('tkgd,tlkd->tkgl', heads_of_queries, heads_of_keys, preferred_...  3.04 us
    another operation x2, local copies, waits for them, and re-layouts, attend(): rows_of_keys.reshape(decode_tokens, -1, KEY_VALUE_HEADS, HEAD_SIZE)  3 us
  transfers between devices with their start and end apart: 9, of which 8 were waited for; matrix products, arithmetic and copies ran while one was open for 20% of the time, Pallas kernels for 0%

profile of v1, /device:TPU:0, one launch (start us, length us, event | category | flops | bytes accessed | tf_op | source)
XLA Modules:
  0.0 98.4 jit_solution(491363810281834953)
XLA Ops:
  0.0 1.0 %convert_reduce_fusion = s32[16]{0:T(128)S(1)} fusion(s32[16]{0:T(128)} %param.22), kind=kLoop, calls=%fused_computation.118 | loop fusion | flops 1264 | bytes 128 | tf_op jit(solution)/shard_map/reduce_sum | solution.py:129
  2.8 2.3 %gather_fusion.1 = bf16[32,2,16,256]{3,2,1,0:T(8,128)(2,1)} fusion(bf16[16,2,16,256]{3,2,1,0:T(8,128)(2,1)} %bitcast.184, s32[1024]{0:T(1024)S(1)} %get-tuple-element.26), kind=kCustom, calls=%fused_computation.1 | custom fusion | bytes 1048704 | tf_op jit(solution)/shard_map/jit(_take)/gather | solution.py:138
  5.1 1.2 %select_select_fusion = bf16[2,16,2,16,256]{4,3,2,1,0:T(8,128)(2,1)S(1)} fusion(bf16[2,16,2,16,256]{4,3,2,1,0:T(8,128)(2,1)} %bitcast.183, pred[2,16]{1,0:T(4,128)(4,1)S(1)} %compare_and_fusion, pred[2,16]{1,0:T(4,128)(4,1)S(1)} %bitcast.196), kind=kLoop, calls=%fused_computation.30 | loop fusion | flops 524288 | bytes 1048640 | tf_op jit(solution)/shard_map/jit(_where)/select_n | solution.py:141
  6.5 0.9 copy.109
  7.4 7.5 %all-to-all-start = ((bf16[16,2,1,2,16,256]{5,4,1,3,2,0:T(8,128)(2,1)}), bf16[16,2,1,2,16,256]{5,4,1,3,2,0:T(8,128)(2,1)}, u32[]{:S(2)}, u32[]{:S(2)}) async-start(bf16[16,2,1,2,16,256]{5,4,1,3,2,0:T(8,128)(2,1)} %copy.109), calls=%async_computation | async-start | bytes 1048576 | tf_op jit(solution)/shard_map/all_to_all | solution.py:21
  14.9 3.1 %gather_fusion.2 = bf16[128,2,16,256]{3,2,1,0:T(8,128)(2,1)} fusion(bf16[32,2,16,256]{3,2,1,0:T(8,128)(2,1)} %param.18, s32[1024]{0:T(1024)S(1)} %get-tuple-element.25), kind=kCustom, calls=%fused_computation.2 | custom fusion | bytes 4194816 | tf_op jit(solution)/shard_map/gather | solution.py:157
  17.9 3.0 %slice_bitcast_fusion.1 = (bf16[8,16,1,16,256]{4,3,1,0,2:T(8,128)(2,1)}, bf16[8,16,1,16,256]{4,3,1,0,2:T(8,128)(2,1)}) fusion(bf16[8,16,2,16,256]{4,3,2,1,0:T(8,128)(2,1)} %bitcast.182), kind=kLoop, calls=%fused_computation.22 | loop fusion | bytes 4194304
  21.0 2.2 %reshape_reshape_squeeze.15 = bf16[8,256,2,128]{3,2,1,0:T(2,128)(2,1)} reshape(bf16[8,16,1,16,256]{4,3,1,0,2:T(8,128)(2,1)} %get-tuple-element.8) | data formatting | bytes 2097152 | tf_op jit(solution)/shard_map/reshape;reshape;squeeze | solution.py:39
  23.2 2.2 %reshape_reshape_squeeze.14 = bf16[8,256,2,128]{3,2,1,0:T(2,128)(2,1)} reshape(bf16[8,16,1,16,256]{4,3,1,0,2:T(8,128)(2,1)} %get-tuple-element.7) | data formatting | bytes 2097152 | tf_op jit(solution)/shard_map/reshape;reshape;squeeze | solution.py:38
  25.7 1.8 %fusion.66 = (f32[8,2,16]{2,1,0:T(2,128)S(1)}, f32[8,2,16,256]{3,2,1,0:T(8,128)S(1)}) fusion(bf16[8,2,16,128]{3,0,2,1:T(8,128)(2,1)S(1)} %bitcast.200, bf16[8,256,2,128]{3,2,1,0:T(2,128)(2,1)} %reshape_reshape_squeeze.14, pred[8,256]{1,0:T(8,128)(4,1)S(1)} %broadcast_compare_fusion), kind=kOutput, calls=%fused_computation.174 | convolution fusion | flops 16973568 | bytes 1379328 | tf_op jit(solution)/shard_map/tkgd,tlkd->tkgl/dot_general | solution.py:43
  29.6 1.1 %iota_compare_fusion.6 = pred[2]{0:T(512)(128)(4,1)} fusion(s32[]{:T(128)} %get-tuple-element.27), kind=kLoop, calls=%fused_computation.167 | loop fusion | flops 2 | bytes 6 | tf_op jit(solution)/shard_map/lt | solution.py:167
  32.5 1.8 %fusion.65 = (bf16[2,16,1,16,256]{4,3,0,2,1:T(8,128)(2,1)}, bf16[2,16,1,16,256]{4,3,0,2,1:T(8,128)(2,1)S(1)}) fusion(bf16[2,16,2,16,256]{4,3,0,2,1:T(8,128)(2,1)} %bitcast.23), kind=kLoop, calls=%fused_computation.173 | loop fusion | bytes 1048576 | tf_op jit(solution)/shard_map/slice | solution.py:144
  35.1 1.0 %copy.110 = bf16[2,16,1,16,256]{4,3,1,0,2:T(8,128)(2,1)S(1)} copy(bf16[2,16,1,16,256]{4,3,0,2,1:T(8,128)(2,1)} %get-tuple-element.9) | data formatting | bytes 524288 | tf_op jit(solution)/shard_map/slice | solution.py:144
  36.9 1.3 %fusion.67 = (f32[2,2,16]{2,1,0:T(2,128)S(1)}, f32[2,2,16,256]{3,2,1,0:T(8,128)S(1)}) fusion(bf16[2,2,16,128]{3,2,1,0:T(8,128)(2,1)} %bitcast.192, bf16[2,256,2,128]{3,2,1,0:T(2,128)(2,1)} %reshape_reshape_squeeze.12, pred[2,256]{1,0:T(4,128)(4,1)} %broadcast_compare_fusion.1), kind=kOutput, calls=%fused_computation.175 | convolution fusion | flops 4243392 | bytes 344832 | tf_op jit(solution)/shard_map/tkgd,tlkd->tkgl/dot_general | solution.py:43
  40.3 1.2 %fusion.10 = bf16[2,2,16,128]{3,2,1,0:T(8,128)(2,1)S(1)} fusion(bf16[2,256,2,128]{3,2,1,0:T(2,128)(2,1)} %reshape_reshape_squeeze.13, f32[2,2,16,256]{3,2,1,0:T(8,128)S(1)} %get-tuple-element.24, f32[2,2,16]{2,1,0:T(2,128)S(1)} %get-tuple-element.18, f32[2,2,16]{2,1,0:T(2,128)S(1)} %multiply_maximum_fusion.1, pred[2,256]{1,0:T(4,128)(4,1)} %broadcast_compare_fusion.1, ...), kind=kOutput, calls=%fused_computation.18 | convolution fusion | flops 4284416 | bytes 347392 | tf_op jit(solution)/shard_map/tkgl,tlkd->tkgd/dot_general | solution.py:64
  44.1 2.8 %collective-permute-start = (bf16[8,4224]{1,0:T(8,128)(2,1)S(1)}, bf16[8,4224]{1,0:T(8,128)(2,1)S(1)}, u32[]{:S(2)}, u32[]{:S(2)}) collective-permute-start(bf16[8,4224]{1,0:T(8,128)(2,1)S(1)} %get-tuple-element.11), channel_id=1, source_target_pairs={{0,8},{1,9},{2,10},{3,11},{4,12},{5,13},{6,14},{7,15},{8,0},{9,1},... | collective-permute-start | bytes 202760 | tf_op jit(solution)/shard_map/ppermute | solution.py:30
  47.0 3.9 %collective-permute-done = bf16[8,4224]{1,0:T(8,128)(2,1)S(1)} collective-permute-done((bf16[8,4224]{1,0:T(8,128)(2,1)S(1)}, bf16[8,4224]{1,0:T(8,128)(2,1)S(1)}, u32[]{:S(2)}, u32[]{:S(2)}) %collective-permute-start) | collective-permute-done | bytes 67616 | tf_op jit(solution)/shard_map/ppermute | solution.py:30
  52.2 3.8 %collective-permute-done.1 = bf16[16,4224]{1,0:T(8,128)(2,1)S(1)} collective-permute-done((bf16[16,4224]{1,0:T(8,128)(2,1)S(1)}, bf16[16,4224]{1,0:T(8,128)(2,1)S(1)}, u32[]{:S(2)}, u32[]{:S(2)}) %collective-permute-start.1) | collective-permute-done | bytes 135200 | tf_op jit(solution)/shard_map/ppermute | solution.py:30
  56.0 1.8 %collective-permute-start.2 = (bf16[32,4224]{1,0:T(8,128)(2,1)S(1)}, bf16[32,4224]{1,0:T(8,128)(2,1)S(1)}, u32[]{:S(2)}, u32[]{:S(2)}) collective-permute-start(bf16[32,4224]{1,0:T(8,128)(2,1)S(1)} %pad_maximum_fusion.1), channel_id=1, source_target_pairs={{0,2},{1,3},{2,0},{3,1},{4,6},{5,7},{6,4},{7,5},{8,10},{9,11},{10,... | collective-permute-start | bytes 811016 | tf_op jit(solution)/shard_map/ppermute | solution.py:30
  58.5 4.0 %collective-permute-done.2 = bf16[32,4224]{1,0:T(8,128)(2,1)S(1)} collective-permute-done((bf16[32,4224]{1,0:T(8,128)(2,1)S(1)}, bf16[32,4224]{1,0:T(8,128)(2,1)S(1)}, u32[]{:S(2)}, u32[]{:S(2)}) %collective-permute-start.2) | collective-permute-done | bytes 270368 | tf_op jit(solution)/shard_map/ppermute | solution.py:30
  63.4 1.2 %collective-permute-done.3 = bf16[64,4224]{1,0:T(8,128)(2,1)S(1)} collective-permute-done((bf16[64,4224]{1,0:T(8,128)(2,1)S(1)}, bf16[64,4224]{1,0:T(8,128)(2,1)S(1)}, u32[]{:S(2)}, u32[]{:S(2)}) %collective-permute-start.3) | collective-permute-done | bytes 540704 | tf_op jit(solution)/shard_map/ppermute | solution.py:30
  66.3 1.9 %fusion.1 = f32[128,384]{1,0:T(8,128)S(1)} fusion(bf16[1,4096,384]{2,1,0:T(8,128)(2,1)S(1)} %copy-done.2, bf16[128,4224]{1,0:T(8,128)(2,1)} %constant_dynamic-update-slice_fusion.16), kind=kOutput, calls=%fused_computation.5 | convolution fusion | flops 402653184 | bytes 4390912 | tf_op jit(solution)/shard_map/dot_general | solution.py:90
  68.2 5.0 %convolution_multiply_fusion = f32[128,4096]{1,0:T(8,128)} fusion(bf16[1,384,4096]{2,1,0:T(8,128)(2,1)S(1)} %copy-done, f32[128]{0:T(128)S(1)} %select_reduce_fusion, f32[128,384]{1,0:T(8,128)S(1)} %fusion.1, bf16[1,4096,384]{2,1,0:T(8,128)(2,1)} %param.26, bf16[128,4224]{1,0:T(8,128)(2,1)} %constant_dynamic-update-slice_fusion.16), kind=kOutput, calls=%fused_computation.3 | convolution fusion | flops 806125568 | bytes 9634304 | tf_op jit(solution)/shard_map/dot_general | solution.py:92
  73.2 1.3 %slice.146 = bf16[64,4096]{1,0:T(8,128)(2,1)S(1)} slice(f32[128,4096]{1,0:T(8,128)} %convolution_multiply_fusion), slice={[64:128], [0:4096]} | slice | bytes 1048576 | tf_op jit(solution)/shard_map/slice | solution.py:95
  74.7 1.8 %collective-permute-done.4 = bf16[64,4096]{1,0:T(8,128)(2,1)S(1)} collective-permute-done((bf16[64,4096]{1,0:T(8,128)(2,1)S(1)}, bf16[64,4096]{1,0:T(8,128)(2,1)S(1)}, u32[]{:S(2)}, u32[]{:S(2)}) %collective-permute-start.4) | collective-permute-done | bytes 524320 | tf_op jit(solution)/shard_map/ppermute | solution.py:30
  76.5 1.3 %slice_add_fusion = f32[64,4096]{1,0:T(8,128)S(1)} fusion(f32[128,4096]{1,0:T(8,128)} %convolution_multiply_fusion, bf16[64,4096]{1,0:T(8,128)(2,1)S(1)} %collective-permute-done.4), kind=kLoop, calls=%fused_computation.20 | loop fusion | flops 524288 | bytes 2621440 | tf_op jit(solution)/shard_map/add | solution.py:96
  77.8 1.8 %collective-permute-start.5 = (bf16[32,4096]{1,0:T(8,128)(2,1)S(1)}, bf16[32,4096]{1,0:T(8,128)(2,1)S(1)}, u32[]{:S(2)}, u32[]{:S(2)}) collective-permute-start(bf16[32,4096]{1,0:T(8,128)(2,1)S(1)} %slice.147), channel_id=1, source_target_pairs={{0,2},{1,3},{2,0},{3,1},{4,6},{5,7},{6,4},{7,5},{8,10},{9,11},{10,... | collective-permute-start | bytes 786440 | tf_op jit(solution)/shard_map/ppermute | solution.py:30
  79.6 6.6 %collective-permute-done.5 = bf16[32,4096]{1,0:T(8,128)(2,1)S(1)} collective-permute-done((bf16[32,4096]{1,0:T(8,128)(2,1)S(1)}, bf16[32,4096]{1,0:T(8,128)(2,1)S(1)}, u32[]{:S(2)}, u32[]{:S(2)}) %collective-permute-start.5) | collective-permute-done | bytes 262176 | tf_op jit(solution)/shard_map/ppermute | solution.py:30
  86.3 2.2 %collective-permute-start.6 = (bf16[16,4096]{1,0:T(8,128)(2,1)S(1)}, bf16[16,4096]{1,0:T(8,128)(2,1)S(1)}, u32[]{:S(2)}, u32[]{:S(2)}) collective-permute-start(bf16[16,4096]{1,0:T(8,128)(2,1)S(1)} %slice.148), channel_id=1, source_target_pairs={{0,4},{1,5},{2,6},{3,7},{4,0},{5,1},{6,2},{7,3},{8,12},{9,13},{10,... | collective-permute-start | bytes 393224 | tf_op jit(solution)/shard_map/ppermute | solution.py:30
  88.5 2.9 %collective-permute-done.6 = bf16[16,4096]{1,0:T(8,128)(2,1)S(1)} collective-permute-done((bf16[16,4096]{1,0:T(8,128)(2,1)S(1)}, bf16[16,4096]{1,0:T(8,128)(2,1)S(1)}, u32[]{:S(2)}, u32[]{:S(2)}) %collective-permute-start.6) | collective-permute-done | bytes 131104 | tf_op jit(solution)/shard_map/ppermute | solution.py:30
  91.5 4.0 %collective-permute-start.7 = (bf16[8,4096]{1,0:T(8,128)(2,1)S(1)}, bf16[8,4096]{1,0:T(8,128)(2,1)S(1)}, u32[]{:S(2)}, u32[]{:S(2)}) collective-permute-start(bf16[8,4096]{1,0:T(8,128)(2,1)S(1)} %slice.149), channel_id=1, source_target_pairs={{0,8},{1,9},{2,10},{3,11},{4,12},{5,13},{6,14},{7,15},{8,0},{9,1},... | collective-permute-start | bytes 196616 | tf_op jit(solution)/shard_map/ppermute | solution.py:30
  95.5 2.2 %collective-permute-done.7 = bf16[8,4096]{1,0:T(8,128)(2,1)S(1)} collective-permute-done((bf16[8,4096]{1,0:T(8,128)(2,1)S(1)}, bf16[8,4096]{1,0:T(8,128)(2,1)S(1)}, u32[]{:S(2)}, u32[]{:S(2)}) %collective-permute-start.7) | collective-permute-done | bytes 65568 | tf_op jit(solution)/shard_map/ppermute | solution.py:30
  (117 shorter events, 18.0 us)
Async XLA Ops:
  0.0 68.2 %copy-start = (bf16[1,384,4096]{2,1,0:T(8,128)(2,1)S(1)}, bf16[1,384,4096]{2,1,0:T(8,128)(2,1)}, u32[]{:S(2)}) copy-start(bf16[1,384,4096]{2,1,0:T(8,128)(2,1)} %param.28) | copy-start | bytes 9437188
  7.4 25.2 %all-to-all-start = ((bf16[16,2,1,2,16,256]{5,4,1,3,2,0:T(8,128)(2,1)}), bf16[16,2,1,2,16,256]{5,4,1,3,2,0:T(8,128)(2,1)}, u32[]{:S(2)}, u32[]{:S(2)}) async-start(bf16[16,2,1,2,16,256]{5,4,1,3,2,0:T(8,128)(2,1)} %copy.109), calls=%async_computation | async-start | bytes 1048576 | tf_op jit(solution)/shard_map/all_to_all | solution.py:21
  23.1 2.2 %copy-start.7 = (bf16[8,2,256]{2,1,0:T(2,128)(2,1)S(1)}, bf16[8,2,256]{2,1,0:T(2,128)(2,1)}, u32[]{:S(2)}) copy-start(bf16[8,2,256]{2,1,0:T(2,128)(2,1)} %param.17) | copy-start | bytes 24580
  23.2 2.3 %copy-start.13 = (s32[8]{0:T(128)S(1)}, s32[8]{0:T(128)}, u32[]{:S(2)}) copy-start(s32[8]{0:T(128)} %param.20) | copy-start | bytes 100
  23.2 2.4 %copy-start.11 = (bf16[8,4096]{1,0:T(8,128)(2,1)S(1)}, bf16[8,4096]{1,0:T(8,128)(2,1)}, u32[]{:S(2)}) copy-start(bf16[8,4096]{1,0:T(8,128)(2,1)} %param.16) | copy-start | bytes 196612
  25.7 2.1 %copy-start.3 = (bf16[8,256,2,128]{3,2,1,0:T(2,128)(2,1)S(1)}, bf16[8,256,2,128]{3,2,1,0:T(2,128)(2,1)}, u32[]{:S(2)}) copy-start(bf16[8,256,2,128]{3,2,1,0:T(2,128)(2,1)} %reshape_reshape_squeeze.15) | copy-start | bytes 3145732
  27.7 1.2 %copy-start.1 = (s32[16]{0:T(128)S(1)}, s32[16]{0:T(128)}, u32[]{:S(2)}) copy-start(s32[16]{0:T(128)} %param.23) | copy-start | bytes 196
  28.1 6.3 %copy-start.4 = (bf16[8,2,16,128]{3,2,1,0:T(8,128)(2,1)}, bf16[8,2,16,128]{3,2,1,0:T(8,128)(2,1)S(1)}, u32[]{:S(2)}) copy-start(bf16[8,2,16,128]{3,2,1,0:T(8,128)(2,1)S(1)} %fusion.7) | copy-start | bytes 196612
  28.9 5.4 %copy-start.10 = (bf16[1,2,32,128]{3,2,1,0:T(8,128)(2,1)}, bf16[1,2,32,128]{3,2,1,0:T(8,128)(2,1)S(1)}, u32[]{:S(2)}) copy-start(bf16[1,2,32,128]{3,2,1,0:T(8,128)(2,1)S(1)} %copy.142) | copy-start | bytes 49156
  35.1 6.4 %slice-start = ((bf16[8,2,16,128]{3,2,1,0:T(8,128)(2,1)}), bf16[2,2,16,128]{3,2,1,0:T(8,128)(2,1)S(1)}, s32[]{:S(2)}) async-start(bf16[8,2,16,128]{3,2,1,0:T(8,128)(2,1)} %copy-done.4), calls=%async_computation.1 | async-start | bytes 32768 | tf_op jit(solution)/shard_map/slice | solution.py:169
  35.1 6.5 %copy-start.5 = (bf16[8,4096]{1,0:T(8,128)(2,1)S(1)}, bf16[8,4096]{1,0:T(8,128)(2,1)}, u32[]{:S(2)}) copy-start(bf16[8,4096]{1,0:T(8,128)(2,1)} %param.15) | copy-start | bytes 196612
  36.9 4.6 %copy-start.12 = (pred[2]{0:T(512)(128)(4,1)S(1)}, pred[2]{0:T(512)(128)(4,1)}, u32[]{:S(2)}) copy-start(pred[2]{0:T(512)(128)(4,1)} %iota_compare_fusion.6) | copy-start | bytes 10
  36.9 4.9 %copy-start.8 = (f32[4096]{0:T(1024)S(1)}, f32[4096]{0:T(1024)}, u32[]{:S(2)}) copy-start(f32[4096]{0:T(1024)} %param.24) | copy-start | bytes 49156
  36.9 5.0 %copy-start.6 = (bf16[4096,8]{0,1:T(8,128)(2,1)S(1)}, bf16[4096,8]{0,1:T(8,128)(2,1)}, u32[]{:S(2)}) copy-start(bf16[4096,8]{0,1:T(8,128)(2,1)} %param.25) | copy-start | bytes 196612
  36.9 5.2 %copy-start.9 = (s32[8,8]{1,0:T(8,128)S(1)}, s32[8,8]{1,0:T(8,128)}, u32[]{:S(2)}) copy-start(s32[8,8]{1,0:T(8,128)} %param.29) | copy-start | bytes 772
  44.1 6.7 %collective-permute-start = (bf16[8,4224]{1,0:T(8,128)(2,1)S(1)}, bf16[8,4224]{1,0:T(8,128)(2,1)S(1)}, u32[]{:S(2)}, u32[]{:S(2)}) collective-permute-start(bf16[8,4224]{1,0:T(8,128)(2,1)S(1)} %get-tuple-element.11), channel_id=1, source_target_pairs={{0,8},{1,9},{2,10},{3,11},{4,12},{5,13},{6,14},{7,15},{8,0},{9,1},... | collective-permute-start | bytes 202760 | tf_op jit(solution)/shard_map/ppermute | solution.py:30
  50.9 5.1 %collective-permute-start.1 = (bf16[16,4224]{1,0:T(8,128)(2,1)S(1)}, bf16[16,4224]{1,0:T(8,128)(2,1)S(1)}, u32[]{:S(2)}, u32[]{:S(2)}) collective-permute-start(bf16[16,4224]{1,0:T(8,128)(2,1)S(1)} %pad_maximum_fusion.2), channel_id=1, source_target_pairs={{0,4},{1,5},{2,6},{3,7},{4,0},{5,1},{6,2},{7,3},{8,12},{9,13},{10,... | collective-permute-start | bytes 405512 | tf_op jit(solution)/shard_map/ppermute | solution.py:30
  56.0 10.3 %copy-start.2 = (bf16[1,4096,384]{2,1,0:T(8,128)(2,1)S(1)}, bf16[1,4096,384]{2,1,0:T(8,128)(2,1)}, u32[]{:S(2)}) copy-start(bf16[1,4096,384]{2,1,0:T(8,128)(2,1)} %param.27) | copy-start | bytes 9437188
  56.0 6.5 %collective-permute-start.2 = (bf16[32,4224]{1,0:T(8,128)(2,1)S(1)}, bf16[32,4224]{1,0:T(8,128)(2,1)S(1)}, u32[]{:S(2)}, u32[]{:S(2)}) collective-permute-start(bf16[32,4224]{1,0:T(8,128)(2,1)S(1)} %pad_maximum_fusion.1), channel_id=1, source_target_pairs={{0,2},{1,3},{2,0},{3,1},{4,6},{5,7},{6,4},{7,5},{8,10},{9,11},{10,... | collective-permute-start | bytes 811016 | tf_op jit(solution)/shard_map/ppermute | solution.py:30
  62.5 2.0 %collective-permute-start.3 = (bf16[64,4224]{1,0:T(8,128)(2,1)S(1)}, bf16[64,4224]{1,0:T(8,128)(2,1)S(1)}, u32[]{:S(2)}, u32[]{:S(2)}) collective-permute-start(bf16[64,4224]{1,0:T(8,128)(2,1)S(1)} %pad_maximum_fusion), channel_id=1, source_target_pairs={{0,1},{1,0},{2,3},{3,2},{4,5},{5,4},{6,7},{7,6},{8,9},{9,8},{10,11... | collective-permute-start | bytes 1622024 | tf_op jit(solution)/shard_map/ppermute | solution.py:30
  74.5 2.0 %collective-permute-start.4 = (bf16[64,4096]{1,0:T(8,128)(2,1)S(1)}, bf16[64,4096]{1,0:T(8,128)(2,1)S(1)}, u32[]{:S(2)}, u32[]{:S(2)}) collective-permute-start(bf16[64,4096]{1,0:T(8,128)(2,1)S(1)} %slice.146), channel_id=1, source_target_pairs={{0,1},{1,0},{2,3},{3,2},{4,5},{5,4},{6,7},{7,6},{8,9},{9,8},{10,11... | collective-permute-start | bytes 1572872 | tf_op jit(solution)/shard_map/ppermute | solution.py:30
  77.8 8.4 %collective-permute-start.5 = (bf16[32,4096]{1,0:T(8,128)(2,1)S(1)}, bf16[32,4096]{1,0:T(8,128)(2,1)S(1)}, u32[]{:S(2)}, u32[]{:S(2)}) collective-permute-start(bf16[32,4096]{1,0:T(8,128)(2,1)S(1)} %slice.147), channel_id=1, source_target_pairs={{0,2},{1,3},{2,0},{3,1},{4,6},{5,7},{6,4},{7,5},{8,10},{9,11},{10,... | collective-permute-start | bytes 786440 | tf_op jit(solution)/shard_map/ppermute | solution.py:30
  86.3 5.1 %collective-permute-start.6 = (bf16[16,4096]{1,0:T(8,128)(2,1)S(1)}, bf16[16,4096]{1,0:T(8,128)(2,1)S(1)}, u32[]{:S(2)}, u32[]{:S(2)}) collective-permute-start(bf16[16,4096]{1,0:T(8,128)(2,1)S(1)} %slice.148), channel_id=1, source_target_pairs={{0,4},{1,5},{2,6},{3,7},{4,0},{5,1},{6,2},{7,3},{8,12},{9,13},{10,... | collective-permute-start | bytes 393224 | tf_op jit(solution)/shard_map/ppermute | solution.py:30
  91.5 6.2 %collective-permute-start.7 = (bf16[8,4096]{1,0:T(8,128)(2,1)S(1)}, bf16[8,4096]{1,0:T(8,128)(2,1)S(1)}, u32[]{:S(2)}, u32[]{:S(2)}) collective-permute-start(bf16[8,4096]{1,0:T(8,128)(2,1)S(1)} %slice.149), channel_id=1, source_target_pairs={{0,8},{1,9},{2,10},{3,11},{4,12},{5,13},{6,14},{7,15},{8,0},{9,1},... | collective-permute-start | bytes 196616 | tf_op jit(solution)/shard_map/ppermute | solution.py:30
